TPU v7x, 32 devices: a whole 2x2x4 slice. The times are simulated.
32 devices in a mesh: rep: 2 (over y), col: 4 (over z), row: 2 (over x), sub: 2 (over core).
Axes of the slice: x: 2, y: 2, z: 4, core: 2. Of those that a mesh axis runs over, the one named last changes fastest.
Arguments:
- node_query: bfloat16 [512, 256], P(('rep', 'row')), parts along dimension 0, may hold values from -6 to 6
- query_angles: float32 [3, 512], P(None, ('rep', 'row')), parts along dimension 1, may hold values from -3.140625 to 3.140625
- query_trans: float32 [3, 512], P(None, ('rep', 'row')), parts along dimension 1, may hold values from -12 to 26
- query_chain: int32 [512], P(('rep', 'row')), parts along dimension 0, may hold values from 0 to 3
- node_key: bfloat16 [2048, 256], P(('rep', 'col', 'row', 'sub')), parts along dimension 0, may hold values from -6 to 6
- key_angles: float32 [3, 2048], P(None, ('rep', 'col')), parts along dimension 1, may hold values from -3.140625 to 3.140625
- key_trans: float32 [3, 2048], P(None, ('rep', 'col')), parts along dimension 1, may hold values from -12 to 12
- key_chain: int32 [2048], P(('rep', 'col')), parts along dimension 0, may hold values from 0 to 3, never falling along the last dimension, each value on 1 to 512 neighbouring positions
- pair_features: bfloat16 [128, 512, 1024], P('sub', ('rep', 'row'), 'col'), parts along dimension 1, may hold values from -6 to 6
- pair_mask: int32 [512, 1024], P(('rep', 'row'), 'col'), parts along dimension 0, may hold values 0 or 1
- query_weight: bfloat16 [256, 336], P(None, 'sub'), may hold values from -0.375 to 0.375
- key_weight: bfloat16 [256, 816], P(None, 'sub'), may hold values from -0.375 to 0.375
- bias_weight: bfloat16 [128, 12], P(None, 'sub'), may hold values from -0.5 to 0.5
- point_gain: float32 [12], P('sub'), may hold values from 0.25 to 2
- chain_gain: float32 [12], P('sub'), may hold values from -2 to 2
- out_weight: bfloat16 [2112, 256], P('sub'), may hold values from -0.125 to 0.125
- first_gain: float32 [256], replicated, may hold values from 0.5 to 1.5
- second_gain: float32 [256], replicated, may hold values from 0.5 to 1.5
- gate_weight: bfloat16 [256, 1024], replicated, may hold values from -0.375 to 0.375
- up_weight: bfloat16 [256, 1024], replicated, may hold values from -0.375 to 0.375
- down_weight: bfloat16 [1024, 256], replicated, may hold values from -0.1875 to 0.1875
- edge_query_weight: bfloat16 [256, 256], replicated, may hold values from -0.375 to 0.375
- edge_key_weight: bfloat16 [256, 256], replicated, may hold values from -0.375 to 0.375
- edge_in_weight: bfloat16 [128, 256], replicated, may hold values from -0.5 to 0.5
- edge_out_weight: bfloat16 [256, 128], replicated, may hold values from -0.375 to 0.375
Outputs:
- updated_nodes: bfloat16 [512, 256], P(('rep', 'row')), parts along dimension 0
- updated_pairs: bfloat16 [128, 512, 1024], P('sub', ('rep', 'row'), 'col'), parts along dimension 1
There are 2 independent parts, one for each index of `rep`. A program takes and returns all parts, laid end to end along the dimension named above; an argument that names none is the same for every part. Nothing has to cross between parts.
All inputs are finite; a program needn't handle non-finite values. No bound on the sum of `pair_mask` on one device may be relied on, other than what follows from the above.
Results may differ from a plain program's by a relative error of at most 0.006.
Values may be sent and summed in bfloat16 or wider, within the bound.
A program may use at most 128 MiB of HBM per device.

v0:
```python
import math

import jax
import jax.numpy as jnp
from jax import lax
from jax.sharding import PartitionSpec as P

CH = 16
PQ = 4
PV = 8


linear_scale = math.sqrt(1.0 / 3.0)
masked_score = -1000000000.0
norm_epsilon = 1e-05


def rotations(angles):
    cos_yaw = jnp.cos(angles[0])
    sin_yaw = jnp.sin(angles[0])
    cos_pitch = jnp.cos(angles[1])
    sin_pitch = jnp.sin(angles[1])
    cos_roll = jnp.cos(angles[2])
    sin_roll = jnp.sin(angles[2])
    first_row = jnp.stack(
        [
            cos_yaw * cos_pitch,
            cos_yaw * sin_pitch * sin_roll - sin_yaw * cos_roll,
            cos_yaw * sin_pitch * cos_roll + sin_yaw * sin_roll,
        ],
        0,
    )
    second_row = jnp.stack(
        [
            sin_yaw * cos_pitch,
            sin_yaw * sin_pitch * sin_roll + cos_yaw * cos_roll,
            sin_yaw * sin_pitch * cos_roll - cos_yaw * sin_roll,
        ],
        0,
    )
    third_row = jnp.stack([-sin_pitch, cos_pitch * sin_roll, cos_pitch * cos_roll], 0)
    return jnp.stack([first_row, second_row, third_row], 0)


def layer_norm(values, gain):
    centred = values - jnp.mean(values, axis=-1, keepdims=True)
    variance = jnp.mean(centred * centred, axis=-1, keepdims=True)
    return centred * lax.rsqrt(variance + norm_epsilon) * gain


def product(left, right):
    return jnp.dot(left, right, preferred_element_type=jnp.float32)


def leading_product(left, right):
    return lax.dot_general(
        left, right, (((0,), (0,)), ((), ())), preferred_element_type=jnp.float32
    )


def row_window(values, begin, count, axis):
    return lax.dynamic_slice_in_dim(values, begin, count, axis)


def finish_nodes(
    sums,
    totals,
    node_rows,
    angle_rows,
    trans_rows,
    out_weight,
    first_gain,
    second_gain,
    gate_weight,
    up_weight,
    down_weight,
):
    row_count, heads = totals.shape
    attended = sums / totals[:, :, None]
    global_points = (
        attended[:, :, CH : CH + 3 * PV].reshape(row_count, heads, 3, PV)
        - trans_rows.T[:, None, :, None]
    )
    local_points = jnp.einsum(
        "bai,ihbp->ihap", rotations(angle_rows), global_points, precision=lax.Precision.HIGHEST
    )
    point_norms = jnp.sqrt(1.0 + jnp.sum(local_points * local_points, axis=2))
    features = jnp.concatenate(
        [
            attended[:, :, :CH],
            local_points.reshape(row_count, heads, 3 * PV),
            point_norms,
            attended[:, :, CH + 3 * PV :],
        ],
        axis=2,
    )
    features = features.reshape(row_count, heads * features.shape[2]).astype(jnp.bfloat16)
    projected = lax.psum(product(features, out_weight), "sub")
    first_nodes = layer_norm(node_rows.astype(jnp.float32) + projected, first_gain)
    first_rounded = first_nodes.astype(jnp.bfloat16)
    hidden = (
        jax.nn.silu(product(first_rounded, gate_weight)) * product(first_rounded, up_weight)
    ).astype(jnp.bfloat16)
    return layer_norm(first_nodes + product(hidden, down_weight), second_gain).astype(jnp.bfloat16)


def attend(
    node_rows,
    angle_rows,
    trans_rows,
    chain_rows,
    mask_rows,
    key_rows,
    key_angles,
    key_trans,
    key_chain,
    tile_pairs,
    query_weight,
    key_weight,
    bias_weight,
    point_gain,
    chain_gain,
):
    highest = lax.Precision.HIGHEST
    heads = point_gain.shape[0]
    query_count, key_count = mask_rows.shape
    query_proj = product(node_rows, query_weight).reshape(query_count, heads, CH + 3 * PQ)
    query_vectors = query_proj[:, :, :CH].astype(jnp.bfloat16)
    query_points = (
        jnp.einsum(
            "abi,ihbp->ihap",
            rotations(angle_rows),
            query_proj[:, :, CH:].reshape(query_count, heads, 3, PQ),
            precision=highest,
        )
        + trans_rows.T[:, None, :, None]
    )
    query_points = query_points.reshape(query_count, heads, 3 * PQ)
    key_proj = product(key_rows, key_weight).reshape(key_count, heads, 2 * CH + 3 * PQ + 3 * PV)
    key_vectors = key_proj[:, :, :CH].astype(jnp.bfloat16)
    value_vectors = key_proj[:, :, CH : 2 * CH].astype(jnp.bfloat16)
    key_frames = rotations(key_angles)
    key_points = (
        jnp.einsum(
            "abi,ihbp->ihap",
            key_frames,
            key_proj[:, :, 2 * CH : 2 * CH + 3 * PQ].reshape(key_count, heads, 3, PQ),
            precision=highest,
        )
        + key_trans.T[:, None, :, None]
    )
    key_points = key_points.reshape(key_count, heads, 3 * PQ)
    value_points = (
        jnp.einsum(
            "abi,ihbp->ihap",
            key_frames,
            key_proj[:, :, 2 * CH + 3 * PQ :].reshape(key_count, heads, 3, PV),
            precision=highest,
        )
        + key_trans.T[:, None, :, None]
    )
    value_points = value_points.reshape(key_count, heads, 3 * PV)
    bias = leading_product(bias_weight, tile_pairs)
    inner = jnp.einsum(
        "ihc,jhc->hij", query_vectors, key_vectors, preferred_element_type=jnp.float32
    ) / math.sqrt(CH)
    cross = jnp.einsum("ihd,jhd->hij", query_points, key_points, precision=highest)
    query_squares = jnp.sum(query_points * query_points, axis=2).T
    key_squares = jnp.sum(key_points * key_points, axis=2).T
    distance = query_squares[:, :, None] + key_squares[:, None, :] - 2.0 * cross
    same_chain = (chain_rows[:, None] == key_chain[None, :]).astype(jnp.float32)
    point_scale = point_gain * (math.sqrt(2.0 / (9.0 * PQ)) / 2.0)
    scores = linear_scale * (
        inner
        + bias
        + chain_gain[:, None, None] * same_chain[None]
        - point_scale[:, None, None] * distance
    )
    scores = jnp.where(mask_rows[None] == 1, scores, masked_score)
    row_max = lax.pmax(jnp.max(scores, axis=2), "col")
    weights = jnp.exp(scores - row_max[:, :, None])
    totals = jnp.sum(weights, axis=2).T
    rounded_weights = weights.astype(jnp.bfloat16)
    vector_part = jnp.einsum(
        "hij,jhc->ihc", rounded_weights, value_vectors, preferred_element_type=jnp.float32
    )
    point_part = jnp.einsum("hij,jhd->ihd", weights, value_points, precision=highest)
    pair_part = lax.dot_general(
        rounded_weights,
        tile_pairs,
        (((2,), (2,)), ((1,), (1,))),
        preferred_element_type=jnp.float32,
    )
    sums = jnp.concatenate([vector_part, point_part, pair_part], axis=2)
    return (totals, sums)


def node_section(
    totals,
    sums,
    node_rows,
    angle_rows,
    trans_rows,
    out_weight,
    first_gain,
    second_gain,
    gate_weight,
    up_weight,
    down_weight,
):
    row_count = node_rows.shape[0]
    share = row_count // lax.axis_size("col")
    begin = lax.axis_index("col") * share
    total_share, sum_share = (
        lax.psum_scatter(totals, "col", scatter_dimension=0, tiled=True),
        lax.psum_scatter(sums, "col", scatter_dimension=0, tiled=True),
    )
    node_share = finish_nodes(
        sum_share,
        total_share,
        row_window(node_rows, begin, share, 0),
        row_window(angle_rows, begin, share, 1),
        row_window(trans_rows, begin, share, 1),
        out_weight,
        first_gain,
        second_gain,
        gate_weight,
        up_weight,
        down_weight,
    )
    return lax.all_gather(node_share, "col", axis=0, tiled=True)


def shards(
    node_query,
    query_angles,
    query_trans,
    query_chain,
    node_key,
    key_angles,
    key_trans,
    key_chain,
    pair_features,
    pair_mask,
    query_weight,
    key_weight,
    bias_weight,
    point_gain,
    chain_gain,
    out_weight,
    first_gain,
    second_gain,
    gate_weight,
    up_weight,
    down_weight,
    edge_query_weight,
    edge_key_weight,
    edge_in_weight,
    edge_out_weight,
):
    key_rows = lax.all_gather(node_key, ("row", "sub"), axis=0, tiled=True)
    query_count = pair_mask.shape[0]
    full_pairs = lax.all_gather(pair_features, "sub", axis=0, tiled=True)
    totals, sums = attend(
        node_query,
        query_angles,
        query_trans,
        query_chain,
        pair_mask,
        key_rows,
        key_angles,
        key_trans,
        key_chain,
        full_pairs,
        query_weight,
        key_weight,
        bias_weight,
        point_gain,
        chain_gain,
    )
    new_nodes = node_section(
        totals,
        sums,
        node_query,
        query_angles,
        query_trans,
        out_weight,
        first_gain,
        second_gain,
        gate_weight,
        up_weight,
        down_weight,
    )
    channel_share = pair_features.shape[0]
    edge_queries = product(new_nodes, edge_query_weight)
    edge_keys = product(key_rows, edge_key_weight)
    out_columns = row_window(
        edge_out_weight, lax.axis_index("sub") * channel_share, channel_share, 1
    )
    block = math.gcd(query_count, 32)

    def edge_step(index, result):
        begin = index * block
        pair_block = row_window(full_pairs, begin, block, 1)
        own_block = row_window(pair_features, begin, block, 1)
        edge_pre = leading_product(edge_in_weight, pair_block)
        edge_pre = (
            edge_pre
            + row_window(edge_queries, begin, block, 0).T[:, :, None]
            + edge_keys.T[:, None, :]
        )
        edge_hidden = jnp.maximum(edge_pre, 0.0).astype(jnp.bfloat16)
        edge_out = leading_product(out_columns, edge_hidden)
        fresh = (own_block.astype(jnp.float32) + edge_out).astype(jnp.bfloat16)
        return lax.dynamic_update_slice_in_dim(result, fresh, begin, 1)

    updated_pairs = lax.fori_loop(0, query_count // block, edge_step, jnp.zeros_like(pair_features))
    return (new_nodes, updated_pairs)


def solution(mesh):
    return jax.shard_map(
        shards,
        mesh=mesh,
        in_specs=(
            P(("rep", "row"), None),
            P(None, ("rep", "row")),
            P(None, ("rep", "row")),
            P(("rep", "row")),
            P(("rep", "col", "row", "sub"), None),
            P(None, ("rep", "col")),
            P(None, ("rep", "col")),
            P(("rep", "col")),
            P("sub", ("rep", "row"), "col"),
            P(("rep", "row"), "col"),
            P(None, "sub"),
            P(None, "sub"),
            P(None, "sub"),
            P("sub"),
            P("sub"),
            P("sub", None),
            P(),
            P(),
            P(),
            P(),
            P(),
            P(),
            P(),
            P(),
            P(),
        ),
        out_specs=(P(("rep", "row"), None), P("sub", ("rep", "row"), "col")),
        check_vma=False,
    )
```

profile of v0, /device:TPU:0, one launch (start us, length us, event | category | flops | bytes accessed | tf_op | source)
XLA Modules:
  0.0 186.0 jit_solution(11751437756029664675)
XLA Ops:
  7.2 6.6 %copy.185 = bf16[64,128,256]{2,0,1:T(8,128)(2,1)} copy(bf16[64,128,256]{2,1,0:T(8,128)(2,1)} %param.35) | data formatting | bytes 8388608 | tf_op args[8]
  13.9 0.6 copy-done.15
  14.6 6.5 %all_gather.9 = bf16[256,256]{1,0:T(8,128)(2,1)S(1)} all-gather(bf16[64,256]{1,0:T(8,128)(2,1)S(1)} %copy-done.15), channel_id=1, replica_groups=mesh['rep'=2,'col'=4,'row'=2,'sub'=2] {'row','sub'}, dimensions={0}, use_global_device_ids=true | all-gather | bytes 163840 | tf_op jit(solution)/shard_map/all_gather | solution.py:261
  21.4 0.8 convert.20
  22.2 0.7 copy.189
  23.5 0.9 copy.215
  25.0 0.6 copy.187
  25.5 4.0 %multiply_reduce_fusion.1 = (f32[128,6]{1,0:T(8,128)}, f32[128,6,3,4]{1,2,3,0:T(4,128)S(1)}) fusion(f32[128,3]{1,0:T(8,128)} %copy.189, f32[128,6,3,4]{1,2,3,0:T(4,128)S(1)} %copy.187, f32[3,3,128,1]{1,0,3,2:T(4,128)} %copy.215), kind=kOutput, calls=%fused_computation.39 | convolution fusion | flops 358656 | bytes 82944 | tf_op jit(solution)/shard_map/abi,ihbp->ihap/dot_general | solution.py:130
  29.5 1.5 copy.190
  31.0 0.4 copy.195
  31.4 0.6 reshape.108
  32.0 1.9 %copy.191 = f32[256,6,3,4]{1,2,3,0:T(4,128)} copy(f32[256,6,3,4]{0,3,2,1:T(4,128)S(1)} %reshape.107) | data formatting | bytes 147456 | tf_op jit(solution)/shard_map/reshape | solution.py:147
  33.9 6.3 %multiply_reduce_fusion = (f32[256,6]{1,0:T(8,128)S(1)}, f32[256,6,3,4]{1,2,3,0:T(4,128)S(1)}) fusion(f32[256,3]{1,0:T(8,128)S(1)} %copy.193, f32[256,6,3,4]{1,2,3,0:T(4,128)} %copy.191, f32[3,3,256,1]{1,0,3,2:T(4,128)S(1)} %copy.216), kind=kOutput, calls=%fused_computation.19 | convolution fusion | flops 717312 | bytes 165888 | tf_op jit(solution)/shard_map/abi,ihbp->ihap/dot_general | solution.py:144
  40.2 0.7 copy.194
  40.9 0.8 copy.196
  41.7 0.9 slice_bitcast_fusion
  42.6 2.7 %copy.197 = f32[256,6,3,8]{3,2,1,0:T(4,128)} copy(f32[256,6,3,8]{0,3,2,1:T(8,128)S(1)} %slice_bitcast_fusion) | data formatting | bytes 294912 | tf_op jit(solution)/shard_map/reshape | solution.py:157
  45.4 8.5 %add_bitcast_fusion = f32[256,6,3,8]{3,2,1,0:T(4,128)} fusion(f32[256,6,3,8]{3,2,1,0:T(4,128)} %copy.197, f32[3,3,256,1]{1,0,3,2:T(4,128)S(1)} %copy.216, f32[256,3]{1,0:T(8,128)S(1)} %copy.193), kind=kOutput, calls=%fused_computation.18 | convolution fusion | flops 1363968 | bytes 307200 | tf_op jit(solution)/shard_map/abi,ihbp->ihap/dot_general | solution.py:154
  53.9 3.0 %copy.200 = f32[256,6,3,8]{0,3,2,1:T(8,128)S(1)} copy(f32[256,6,3,8]{3,2,1,0:T(4,128)} %add_bitcast_fusion) | data formatting | bytes 294912 | tf_op jit(solution)/shard_map/add | solution.py:154
  57.1 0.9 fusion.30
  58.1 4.6 %fusion.63 = f32[6,128,256]{2,0,1:T(8,128)S(1)} fusion(bf16[128,128,256]{2,0,1:T(8,128)(2,1)} %all-gather.2.cloned.1.call-done, bf16[128,6]{0,1:T(8,128)(2,1)S(1)} %copy-done.23), kind=kOutput, calls=%fused_computation.91 | convolution fusion | flops 50331648 | bytes 9176576 | tf_op jit(solution)/shard_map/dot_general | solution.py:56
  62.7 1.5 fusion.83
  64.1 12.4 %pmax.7 = f32[6,128]{1,0:T(8,128)S(1)} all-reduce(f32[6,128]{1,0:T(8,128)S(1)} %get-tuple-element.252), channel_id=1, replica_groups=mesh['rep'=2,'col'=4,'row'=2,'sub'=2] {'col'}, use_global_device_ids=true, to_apply=%region_3.4 | all-reduce | flops 768 | bytes 6144 | tf_op jit(solution)/shard_map/pmax | solution.py:180
  76.5 0.3 fusion.34
  76.8 0.9 convolution_bitcast_fusion
  77.7 1.0 convolution_bitcast_fusion.1
  78.7 0.7 copy.228
  80.0 5.7 %fusion.36 = f32[128,6,128]{2,1,0:T(8,128)S(1)} fusion(bf16[128,128,256]{2,0,1:T(8,128)(2,1)} %all-gather.2.cloned.1.call-done, bf16[6,128,256]{2,1,0:T(8,128)(2,1)S(1)} %get-tuple-element.221), kind=kOutput, calls=%fused_computation.43 | convolution fusion | flops 50331648 | bytes 9175040 | tf_op jit(solution)/shard_map/dot_general | solution.py:188
  85.7 1.6 pad_maximum_fusion
  88.1 9.0 %reduce-scatter.7.cloned.1.call-done = f32[32,6]{1,0:T(8,128)} async-done(((f32[128,6]{1,0:T(8,128)}), f32[32,6]{1,0:T(8,128)}) %reduce-scatter.7.cloned.1.call-update) | async-done | bytes 784
  97.1 0.8 copy.229
  97.9 27.6 %reduce-scatter.5.cloned.1.call-done = f32[32,6,168]{2,1,0:T(8,128)} async-done(((f32[128,6,168]{2,1,0:T(8,128)}), f32[32,6,168]{2,1,0:T(8,128)}) %reduce-scatter.5.cloned.1.call-update) | async-done | bytes 129040 | tf_op jit(solution)/shard_map/reduce_scatter | solution.py:216
  125.5 1.2 copy.204
  127.0 1.0 convert_bitcast_fusion
  128.6 3.4 %psum.7 = f32[32,256]{1,0:T(8,128)S(1)} all-reduce(f32[32,256]{1,0:T(8,128)S(1)} %fusion.89), channel_id=1, replica_groups=mesh['rep'=2,'col'=4,'row'=2,'sub'=2] {'sub'}, use_global_device_ids=true, to_apply=%region_8.9 | all-reduce | flops 8192 | bytes 65536 | tf_op jit(solution)/shard_map/psum | solution.py:98
  132.6 1.6 fusion.84
  134.5 13.2 %all_gather.11 = bf16[128,256]{1,0:T(8,128)(2,1)S(1)} all-gather(bf16[32,256]{1,0:T(8,128)(2,1)S(1)} %multiply_convert_fusion), channel_id=1, replica_groups=mesh['rep'=2,'col'=4,'row'=2,'sub'=2] {'col'}, dimensions={0}, use_global_device_ids=true | all-gather | bytes 81920 | tf_op jit(solution)/shard_map/all_gather | solution.py:231
  147.9 2.5 %broadcast_in_dim.20.clone = bf16[64,128,256]{2,1,0:T(8,128)(2,1)} broadcast(bf16[]{:T(256)} %constant.79.clone.1), dimensions={} | broadcast | bytes 4194306 | tf_op jit(solution)/shard_map/broadcast_in_dim | solution.py:317
  150.4 28.4 %while.13 = (s32[]{:T(128)}, bf16[64,128,256]{2,1,0:T(8,128)(2,1)}, bf16[64,128,256]{2,0,1:T(8,128)(2,1)}, bf16[128,128,256]{2,0,1:T(8,128)(2,1)}, bf16[128,256]...) while((s32[]{:T(128)}, bf16[64,128,256]{2,1,0:T(8,128)(2,1)}, ...), condition=%wide.region_14.15_spmd, body=%wide.region_13.14_spmd.sunk | while | flops 815267840 | bytes 6751403 | solution.py:317
  150.4 5.5 %fusion.127 = bf16[64,32,256]{2,0,1:T(8,128)(2,1)S(1)} fusion(f32[256,256]{0,1:T(8,128)S(1)} %bitcast.137, f32[256,32]{0,1:T(8,128)S(1)} %dynamic-slice_bitcast_fusion.3, bf16[128,128,256]{2,0,1:T(8,128)(2,1)} %get-tuple-element.340, s32[]{:T(128)S(6)} %select_n.27, bf16[64,128,256]{2,0,1:T(8,128)(2,1)} %get-tuple-element.339, ...), kind=kOutput, calls=%fused_computation.10.clone.1 | convolution fusion | flops 815267840 | bytes 4588544 | tf_op jit(solution)/shard_map/while/body/eval_jaxpr/dot_general | solution.py:56
  155.9 1.6 copy_dynamic-update-slice_fusion.2
  157.5 5.5 %fusion.127 = bf16[64,32,256]{2,0,1:T(8,128)(2,1)S(1)} fusion(f32[256,256]{0,1:T(8,128)S(1)} %bitcast.137, f32[256,32]{0,1:T(8,128)S(1)} %dynamic-slice_bitcast_fusion.3, bf16[128,128,256]{2,0,1:T(8,128)(2,1)} %get-tuple-element.340, s32[]{:T(128)S(6)} %select_n.27, bf16[64,128,256]{2,0,1:T(8,128)(2,1)} %get-tuple-element.339, ...), kind=kOutput, calls=%fused_computation.10.clone.1 | convolution fusion | flops 815267840 | bytes 4588544 | tf_op jit(solution)/shard_map/while/body/eval_jaxpr/dot_general | solution.py:56
  163.0 1.6 copy_dynamic-update-slice_fusion.2
  164.6 5.5 %fusion.127 = bf16[64,32,256]{2,0,1:T(8,128)(2,1)S(1)} fusion(f32[256,256]{0,1:T(8,128)S(1)} %bitcast.137, f32[256,32]{0,1:T(8,128)S(1)} %dynamic-slice_bitcast_fusion.3, bf16[128,128,256]{2,0,1:T(8,128)(2,1)} %get-tuple-element.340, s32[]{:T(128)S(6)} %select_n.27, bf16[64,128,256]{2,0,1:T(8,128)(2,1)} %get-tuple-element.339, ...), kind=kOutput, calls=%fused_computation.10.clone.1 | convolution fusion | flops 815267840 | bytes 4588544 | tf_op jit(solution)/shard_map/while/body/eval_jaxpr/dot_general | solution.py:56
  170.1 1.6 copy_dynamic-update-slice_fusion.2
  171.7 5.5 %fusion.127 = bf16[64,32,256]{2,0,1:T(8,128)(2,1)S(1)} fusion(f32[256,256]{0,1:T(8,128)S(1)} %bitcast.137, f32[256,32]{0,1:T(8,128)S(1)} %dynamic-slice_bitcast_fusion.3, bf16[128,128,256]{2,0,1:T(8,128)(2,1)} %get-tuple-element.340, s32[]{:T(128)S(6)} %select_n.27, bf16[64,128,256]{2,0,1:T(8,128)(2,1)} %get-tuple-element.339, ...), kind=kOutput, calls=%fused_computation.10.clone.1 | convolution fusion | flops 815267840 | bytes 4588544 | tf_op jit(solution)/shard_map/while/body/eval_jaxpr/dot_general | solution.py:56
  177.2 1.6 copy_dynamic-update-slice_fusion.2
  178.8 0.6 copy.248
  (130 shorter events, 4.8 us)
Async XLA Ops:
  7.2 121.2 %copy-start = (bf16[1056,256]{1,0:T(8,128)(2,1)S(1)}, bf16[1056,256]{1,0:T(8,128)(2,1)}, u32[]{:S(2)}) copy-start(bf16[1056,256]{1,0:T(8,128)(2,1)} %param.42) | copy-start | bytes 1622020
  7.2 50.9 %all-gather.2.cloned.1.call-start = ((), (), s32[]{:S(2)}) async-start(), calls=%async_computation.2 | async-start | bytes 12582912 | tf_op jit(solution)/shard_map/all_gather | solution.py:263
  13.8 0.8 copy-start.15
  13.8 7.3 %copy-start.5 = (bf16[256,408]{0,1:T(8,128)(2,1)S(1)}, bf16[256,408]{0,1:T(8,128)(2,1)}, u32[]{:S(2)}) copy-start(bf16[256,408]{0,1:T(8,128)(2,1)} %param.38) | copy-start | bytes 626692
  13.8 8.4 %copy-start.20 = (f32[3,128]{1,0:T(4,128)S(1)}, f32[3,128]{1,0:T(4,128)}, u32[]{:S(2)}) copy-start(f32[3,128]{1,0:T(4,128)} %param.29) | copy-start | bytes 4612
  13.8 9.1 %copy-start.6 = (bf16[128,256]{1,0:T(8,128)(2,1)S(1)}, bf16[128,256]{1,0:T(8,128)(2,1)}, u32[]{:S(2)}) copy-start(bf16[128,256]{1,0:T(8,128)(2,1)} %param.27) | copy-start | bytes 196612
  13.8 9.1 %copy-start.12 = (bf16[256,168]{0,1:T(8,128)(2,1)S(1)}, bf16[256,168]{0,1:T(8,128)(2,1)}, u32[]{:S(2)}) copy-start(bf16[256,168]{0,1:T(8,128)(2,1)} %param.37) | copy-start | bytes 258052
  13.8 9.4 %copy-start.22 = (f32[3,256]{1,0:T(4,128)S(1)}, f32[3,256]{1,0:T(4,128)}, u32[]{:S(2)}) copy-start(f32[3,256]{1,0:T(4,128)} %param.33) | copy-start | bytes 9220
  13.8 9.5 %copy-start.17 = (f32[3,128]{1,0:T(4,128)S(1)}, f32[3,128]{1,0:T(4,128)}, u32[]{:S(2)}) copy-start(f32[3,128]{1,0:T(4,128)} %param.28) | copy-start | bytes 4612
  13.8 10.6 %copy-start.19 = (f32[3,256]{1,0:T(4,128)S(1)}, f32[3,256]{1,0:T(4,128)}, u32[]{:S(2)}) copy-start(f32[3,256]{1,0:T(4,128)} %param.32) | copy-start | bytes 9220
  13.9 83.2 %reduce-scatter.7.cloned.1.call-start = ((), (), s32[]{:S(2)}) async-start(), calls=%async_computation.4 | async-start | bytes 81920
  21.4 3.6 %copy-start.1 = (f32[256,6,68]{0,2,1:T(8,128)}, f32[256,6,68]{0,2,1:T(8,128)S(1)}, u32[]{:S(2)}) copy-start(f32[256,6,68]{0,2,1:T(8,128)S(1)} %reshape.104) | copy-start | bytes 1253380
  23.1 1.8 copy-start.3
  45.3 11.6 %copy-start.18 = (f32[3,128]{1,0:T(4,128)S(1)}, f32[3,128]{1,0:T(4,128)}, u32[]{:S(2)}) copy-start(f32[3,128]{1,0:T(4,128)} %param.28) | copy-start | bytes 4612
  45.3 11.6 %copy-start.21 = (f32[3,128]{1,0:T(4,128)S(1)}, f32[3,128]{1,0:T(4,128)}, u32[]{:S(2)}) copy-start(f32[3,128]{1,0:T(4,128)} %param.29) | copy-start | bytes 4612
  45.3 11.7 %copy-start.31 = (f32[6]{0:T(128)S(1)}, f32[6]{0:T(128)}, u32[]{:S(2)}) copy-start(f32[6]{0:T(128)} %param.40) | copy-start | bytes 76
  45.3 11.7 %copy-start.9 = (s32[128,256]{1,0:T(8,128)S(1)}, s32[128,256]{1,0:T(8,128)}, u32[]{:S(2)}) copy-start(s32[128,256]{1,0:T(8,128)} %param.36) | copy-start | bytes 393220
  45.3 11.7 %copy-start.24 = (s32[256]{0:T(256)S(1)}, s32[256]{0:T(256)}, u32[]{:S(2)}) copy-start(s32[256]{0:T(256)} %param.34) | copy-start | bytes 3076
  45.3 11.7 %copy-start.27 = (s32[128]{0:T(128)S(1)}, s32[128]{0:T(128)}, u32[]{:S(2)}) copy-start(s32[128]{0:T(128)} %param.30) | copy-start | bytes 1540
  45.3 11.8 %copy-start.8 = (f32[128,6,12]{0,2,1:T(8,128)S(1)}, f32[128,6,12]{0,2,1:T(8,128)}, u32[]{:S(2)}) copy-start(f32[128,6,12]{0,2,1:T(8,128)} %reshape.108) | copy-start | bytes 110596
  45.3 11.8 %copy-start.14 = (f32[6,256]{1,0:T(8,128)S(1)}, f32[6,256]{1,0:T(8,128)}, u32[]{:S(2)}) copy-start(f32[6,256]{1,0:T(8,128)} %copy.194) | copy-start | bytes 18436
  45.3 11.8 %copy-start.16 = (f32[6,128]{1,0:T(8,128)S(1)}, f32[6,128]{1,0:T(8,128)}, u32[]{:S(2)}) copy-start(f32[6,128]{1,0:T(8,128)} %copy.190) | copy-start | bytes 9220
  45.3 12.7 %copy-start.23 = (bf16[128,6]{0,1:T(8,128)(2,1)S(1)}, bf16[128,6]{0,1:T(8,128)(2,1)}, u32[]{:S(2)}) copy-start(bf16[128,6]{0,1:T(8,128)(2,1)} %param.39) | copy-start | bytes 4612
  58.0 4.6 %copy-start.4 = (f32[128,6,28]{0,2,1:T(8,128)S(1)}, f32[128,6,28]{0,2,1:T(8,128)}, u32[]{:S(2)}) copy-start(f32[128,6,28]{0,2,1:T(8,128)} %copy-done.3) | copy-start | bytes 258052
  58.0 4.6 %copy-start.28 = (f32[6]{0:T(128)S(1)}, f32[6]{0:T(128)}, u32[]{:S(2)}) copy-start(f32[6]{0:T(128)} %param.41) | copy-start | bytes 76
  79.5 46.0 %reduce-scatter.5.cloned.1.call-start = ((), (), s32[]{:S(2)}) async-start(), calls=%async_computation.3 | async-start | bytes 1310720 | tf_op jit(solution)/shard_map/reduce_scatter | solution.py:216
  80.0 7.7 %copy-start.13 = (bf16[256,128]{1,0:T(8,128)(2,1)S(1)}, bf16[256,128]{1,0:T(8,128)(2,1)}, u32[]{:S(2)}) copy-start(bf16[256,128]{1,0:T(8,128)(2,1)} %param.51) | copy-start | bytes 196612
  80.0 7.8 %copy-start.11 = (bf16[256,256]{1,0:T(8,128)(2,1)S(1)}, bf16[256,256]{1,0:T(8,128)(2,1)}, u32[]{:S(2)}) copy-start(bf16[256,256]{1,0:T(8,128)(2,1)} %param.49) | copy-start | bytes 393220
  87.3 44.8 %copy-start.7 = (bf16[128,256]{1,0:T(8,128)(2,1)S(1)}, bf16[128,256]{1,0:T(8,128)(2,1)}, u32[]{:S(2)}) copy-start(bf16[128,256]{1,0:T(8,128)(2,1)} %param.27) | copy-start | bytes 196612
  87.3 45.1 %copy-start.2 = (bf16[256,1024]{1,0:T(8,128)(2,1)S(1)}, bf16[256,1024]{1,0:T(8,128)(2,1)}, u32[]{:S(2)}) copy-start(bf16[256,1024]{1,0:T(8,128)(2,1)} %param.45) | copy-start | bytes 1572868
  87.3 45.1 %copy-start.25 = (f32[256]{0:T(256)S(1)}, f32[256]{0:T(256)}, u32[]{:S(2)}) copy-start(f32[256]{0:T(256)} %param.43) | copy-start | bytes 3076
  87.3 45.3 %copy-start.29 = (bf16[1024,256]{1,0:T(8,128)(2,1)S(1)}, bf16[1024,256]{1,0:T(8,128)(2,1)}, u32[]{:S(2)}) copy-start(bf16[1024,256]{1,0:T(8,128)(2,1)} %param.47) | copy-start | bytes 1572868
  87.9 46.6 %copy-start.26 = (f32[256]{0:T(256)S(1)}, f32[256]{0:T(256)}, u32[]{:S(2)}) copy-start(f32[256]{0:T(256)} %param.44) | copy-start | bytes 3076
  88.1 59.7 %copy-start.10 = (bf16[256,256]{1,0:T(8,128)(2,1)S(1)}, bf16[256,256]{1,0:T(8,128)(2,1)}, u32[]{:S(2)}) copy-start(bf16[256,256]{1,0:T(8,128)(2,1)} %param.48) | copy-start | bytes 393220
  128.3 22.1 %copy-start.30 = (bf16[128,256]{1,0:T(8,128)(2,1)S(1)}, bf16[128,256]{1,0:T(8,128)(2,1)}, u32[]{:S(2)}) copy-start(bf16[128,256]{1,0:T(8,128)(2,1)} %param.50) | copy-start | bytes 196612
Sparse Core Ops, SparseCore 0:
  14.0 22.5 all-gather.1
  79.6 17.4 reduce-scatter.6
  99.9 25.4 reduce-scatter.4
where the time goes:
time: 187 us; the launch traced here: 186 us
  matrix products  59.1 us (32%)
  waiting for transfers between devices  36.7 us (20%)
  local copies, waits for them, and re-layouts  35.9 us (19%)
  blocking collectives  35.5 us (19%)
  between operations  14.5 us (8%)
  other arithmetic  4.1 us (2%)
    reduce_scatter x1, waiting for transfers between devices, node_section(): lax.psum_scatter(sums, 'col', scatter_dimension=0, tiled=True)  27.6 us
    dot_general x5, matrix products, leading_product(): lax.dot_general(left, right, (((0,), (0,)), ((), ())), preferred_element_...  26.7 us
    all_gather x1, blocking collectives, node_section(): return lax.all_gather(node_share, 'col', axis=0, tiled=True)  13.2 us
    pmax x1, blocking collectives, attend(): row_max = lax.pmax(jnp.max(scores, axis=2), 'col')  12.4 us
    unnamed x69, local copies, waits for them, and re-layouts  9.61 us
    unnamed x4, waiting for transfers between devices  9.05 us
    dot_general x1, matrix products, attend(): jnp.einsum('abi,ihbp->ihap', key_frames, key_proj[:, :, 2 * CH + 3 * PQ:]...  8.52 us
    all_gather x1, blocking collectives, shards(): key_rows = lax.all_gather(node_key, ('row', 'sub'), axis=0, tiled=True)  6.49 us
  transfers between devices with their start and end apart: 3, of which 2 were waited for; matrix products, arithmetic and copies ran while one was open for 25% of the time, Pallas kernels for 0%

commit v1 on v0

v1 whole, which is shorter than its diff:
```python
import functools
import math

import jax
import jax.numpy as jnp
from jax import lax
from jax.experimental import pallas as pl
from jax.experimental.pallas import tpu as pltpu
from jax.sharding import PartitionSpec as P

CH = 16
PQ = 4
PV = 8

linear_scale = math.sqrt(1.0 / 3.0)
masked_score = -1000000000.0
norm_epsilon = 1e-05
ROWS = 16
SLOT = 16
DEPTH = 40
SMALL = CH + 4 * PV

MESH = pl.DeviceIdType.MESH
HIGH = lax.Precision.HIGHEST
F32 = jnp.float32
BF16 = jnp.bfloat16


def rotation_rows(angles):
    cy, sy = jnp.cos(angles[0:1]), jnp.sin(angles[0:1])
    cp, sp = jnp.cos(angles[1:2]), jnp.sin(angles[1:2])
    cr, sr = jnp.cos(angles[2:3]), jnp.sin(angles[2:3])
    return (
        (cy * cp, cy * sp * sr - sy * cr, cy * sp * cr + sy * sr),
        (sy * cp, sy * sp * sr + cy * cr, sy * sp * cr - cy * sr),
        (-sp, cp * sr, cp * cr),
    )


def layer_norm(values, gain):
    centred = values - jnp.mean(values, axis=-1, keepdims=True)
    variance = jnp.mean(centred * centred, axis=-1, keepdims=True)
    return centred * lax.rsqrt(variance + norm_epsilon) * gain


def dot(left, right, dims=(((1,), (0,)), ((), ())), precision=None):
    return lax.dot_general(left, right, dims, precision=precision, preferred_element_type=F32)


def take_rows(ref, rows):
    return jnp.concatenate([ref[t, rows, :] for t in range(ref.shape[0])], axis=1)


def put_rows(ref, rows, values):
    for t in range(ref.shape[0]):
        ref[t, rows, :] = values[:, t * 128 : (t + 1) * 128]


NT = (((1,), (1,)), ((), ()))
TN = (((0,), (0,)), ((), ()))


def kernel(
    dims,
    nq_ref, qa_ref, qt_ref, qc_ref, nk_ref, ka_ref, kt_ref, kc_ref, pair_ref, mask_ref,
    wq_ref, wk_ref, wb_ref, pg_ref, cg_ref, wo_ref, g1_ref, g2_ref,
    gate_hbm, up_hbm, down_hbm, weq_ref, wek_ref, wei_ref, weo_ref,
    nodes_ref, pairs_ref,
    xin, xown, keys, wq2, wk2, wb2, pg2, cg2, wo2, gate, up, down,
    padk, padq, padb, amat, bmat, vvec, vpts, ekt, lhs_in, lhs_out,
    xf, xt, sc_ref, pv_ref, s_ref, stat_send, stat_recv, fmat, lpmat, wsmall, wnorm, nq3,
    psend, precv, nsend, eqf, ostage, rstage,
    sem_in, sem_out, sem_own, key_s, key_r, w_s, w_r, ffn_sem, stat_s, stat_r,
    red_s, red_r, ag_s, ag_r, node_s, node_r, o_own, o_s, o_r,
):
    S, R, C, heads_local, half, kcount, share, channels = dims
    heads = heads_local * S
    blocks = half // ROWS
    s, row, col = lax.axis_index("sub"), lax.axis_index("row"), lax.axis_index("col")
    other = 1 - s

    barrier = pltpu.get_barrier_semaphore()
    group = [(dr, ds) for dr in range(R) for ds in range(S) if (dr, ds) != (0, 0)]

    def near(dr, ds):
        return {"row": lax.rem(row + dr, R), "sub": lax.rem(s + ds, S)}

    def along(dc):
        return {"col": lax.rem(col + dc, C)}

    for dr, ds in group:
        pl.semaphore_signal(barrier, inc=1, device_id=near(dr, ds), device_id_type=MESH)
    for dc in range(1, C):
        pl.semaphore_signal(barrier, inc=1, device_id=along(dc), device_id_type=MESH)
    pl.semaphore_wait(barrier, len(group) + C - 1)

    def remote(src, dst, send, recv, device):
        return pltpu.make_async_remote_copy(
            src_ref=src, dst_ref=dst, send_sem=send, recv_sem=recv,
            device_id=device, device_id_type=MESH,
        )

    key_copies = []
    for n, (dr, ds) in enumerate(group):
        copy = remote(nk_ref, keys.at[row * S + s], key_s.at[n], key_r.at[n], near(dr, ds))
        copy.start()
        key_copies.append(copy)
    weight_copies = []
    for n, (src, dst) in enumerate(
        ((wk_ref, wk2), (wq_ref, wq2), (wb_ref, wb2), (pg_ref, pg2), (cg_ref, cg2), (wo_ref, wo2))
    ):
        copy = remote(src, dst.at[s], w_s.at[n], w_r.at[n], {"sub": other})
        copy.start()
        weight_copies.append(copy)
    pair_copies = []
    own_copies = []
    for b in range(blocks):
        copy = remote(
            pair_ref.at[:, pl.ds(other * half + b * ROWS, ROWS), :],
            xin.at[b], sem_out.at[b], sem_in.at[b], {"sub": other},
        )
        copy.start()
        pair_copies.append(copy)
        copy = pltpu.make_async_copy(
            pair_ref.at[:, pl.ds(s * half + b * ROWS, ROWS), :], xown.at[b], sem_own.at[b]
        )
        copy.start()
        own_copies.append(copy)
    ffn_copies = []
    for n, (src, dst) in enumerate(((gate_hbm, gate), (up_hbm, up), (down_hbm, down))):
        copy = pltpu.make_async_copy(src, dst, ffn_sem.at[n])
        copy.start()
        ffn_copies.append(copy)
    keys[row * S + s] = nk_ref[...]
    wk2[s] = wk_ref[...]
    wq2[s] = wq_ref[...]
    wb2[s] = wb_ref[...]
    pg2[s] = pg_ref[...]
    cg2[s] = cg_ref[...]
    wo2[s] = wo_ref[...]

    kr = rotation_rows(ka_ref[...])
    kt = kt_ref[...]
    kcv = kc_ref[...]

    def pick(values):
        return jnp.where(s == 0, values[:, :half], values[:, half:])

    qr = rotation_rows(pick(qa_ref[...]))
    qt = pick(qt_ref[...])
    qcv = pick(qc_ref[...])

    for copy in weight_copies:
        copy.wait()
    for copy in key_copies:
        copy.wait()

    kall = keys[...].reshape(kcount, keys.shape[2])
    kwide = 2 * CH + 3 * PQ + 3 * PV
    qwide = CH + 3 * PQ
    point_scale = math.sqrt(2.0 / (9.0 * PQ)) / 2.0
    for hs in range(S):
        padk[:, : wk2.shape[2]] = dot(kall, wk2[hs])
        kp = padk[...].T
        padq[:, : wq2.shape[2]] = dot(nq_ref[...], wq2[hs])
        qp = pick(padq[...].T)
        for k in range(heads_local):
            h = hs * heads_local + k
            base = k * kwide
            bmat[h, 0:CH] = kp[base : base + CH].astype(BF16).astype(F32)
            vvec[h] = kp[base + CH : base + 2 * CH].astype(BF16)
            norm = jnp.zeros((1, kcount), F32)
            for a in range(3):
                g = kt[a : a + 1] + jnp.zeros((PQ, kcount), F32)
                v = kt[a : a + 1] + jnp.zeros((PV, kcount), F32)
                for b in range(3):
                    at = base + 2 * CH + b * PQ
                    g = g + kr[a][b] * kp[at : at + PQ]
                    at = base + 2 * CH + 3 * PQ + b * PV
                    v = v + kr[a][b] * kp[at : at + PV]
                bmat[h, CH + a * PQ : CH + a * PQ + PQ] = g
                vpts[h, a * PV : a * PV + PV] = v
                norm = norm + jnp.sum(g * g, axis=0, keepdims=True)
            top = CH + 3 * PQ
            bmat[h, top : top + 1] = jnp.ones((1, kcount), F32)
            bmat[h, top + 1 : top + 2] = norm
            for c in range(4):
                bmat[h, top + 2 + c : top + 3 + c] = (kcv == c).astype(F32)
            bmat[h, top + 6 :] = jnp.zeros((DEPTH - top - 6, kcount), F32)

            base = k * qwide
            gain = pg2[hs][:, k : k + 1] * (point_scale * linear_scale)
            chain = cg2[hs][:, k : k + 1] * linear_scale
            amat[h, 0:CH] = qp[base : base + CH].astype(BF16).astype(F32) * (
                linear_scale / math.sqrt(CH)
            )
            norm = jnp.zeros((1, half), F32)
            for a in range(3):
                g = qt[a : a + 1] + jnp.zeros((PQ, half), F32)
                for b in range(3):
                    at = base + CH + b * PQ
                    g = g + qr[a][b] * qp[at : at + PQ]
                amat[h, CH + a * PQ : CH + a * PQ + PQ] = g * (2.0 * gain)
                norm = norm + jnp.sum(g * g, axis=0, keepdims=True)
            amat[h, top : top + 1] = -gain * norm
            amat[h, top + 1 : top + 2] = -gain + jnp.zeros((1, half), F32)
            for c in range(4):
                amat[h, top + 2 + c : top + 3 + c] = jnp.where(qcv == c, chain, 0.0)
            amat[h, top + 6 :] = jnp.zeros((DEPTH - top - 6, half), F32)

    padb[...] = jnp.zeros(padb.shape, F32)
    for hs in range(S):
        padb[0:channels, hs * heads_local : (hs + 1) * heads_local] = wb2[hs].astype(F32)
    bias_left = (padb[...].T[0:SLOT] * linear_scale)
    bias_hi = bias_left.astype(BF16)
    bias_lo = (bias_left - bias_hi.astype(F32)).astype(BF16)
    bias_left = jnp.concatenate([bias_hi, bias_lo], axis=0)
    ekt[...] = dot(kall, wek_ref[...]).T
    lhs_in[:, 0:channels] = wei_ref[...].astype(F32).T.astype(BF16)
    lhs_out[...] = weo_ref[...].astype(F32).T.astype(BF16)

    cs = channels // S
    own_rows = pl.ds(pl.multiple_of(s * (cs * ROWS), cs * ROWS), cs * ROWS)
    other_rows = pl.ds(pl.multiple_of(other * (cs * ROWS), cs * ROWS), cs * ROWS)
    for b in range(blocks):
        own_copies[b].wait()
        pair_copies[b].wait()
        put_rows(xf, own_rows, xown[b].astype(F32).reshape(cs * ROWS, kcount))
        put_rows(xf, other_rows, xin[b].astype(F32).reshape(cs * ROWS, kcount))
        for i in range(ROWS):
            block = take_rows(xf, pl.ds(i, channels, stride=ROWS)).astype(BF16)
            xt[b * ROWS + i] = block
            both = dot(bias_left, block)
            at = (b * ROWS + i) * SLOT
            put_rows(sc_ref, pl.ds(at, SLOT), both[0:SLOT] + both[SLOT:])

    valid = mask_ref[pl.ds(pl.multiple_of(s * half, half), half), :] == 1
    lane = lax.broadcasted_iota(jnp.int32, (half, 128), 1)
    stats = jnp.zeros((half, 128), F32)
    for h in range(heads):
        scores = dot(amat[h], bmat[h], TN, HIGH)
        scores = scores + take_rows(sc_ref, pl.ds(h, half, stride=SLOT))
        scores = jnp.where(valid, scores, masked_score)
        top = jnp.max(scores, axis=1, keepdims=True)
        weights = jnp.exp(scores - top)
        total = jnp.sum(weights, axis=1, keepdims=True)
        rounded = weights.astype(BF16)
        put_rows(sc_ref, pl.ds(h, half, stride=SLOT), rounded.astype(F32))
        stats = jnp.where(lane == h, top, stats)
        stats = jnp.where(lane == SLOT + h, total, stats)
        pv_ref[h, 0:CH] = dot(vvec[h], rounded, NT)
        pv_ref[h, CH:] = dot(vpts[h], weights, NT, HIGH)
    padb[0:half] = stats
    stat_send[...] = padb[...].T[0 : 2 * SLOT]
    stat_copies = []
    for dc in range(1, C):
        copy = remote(stat_send, stat_recv.at[dc], stat_s.at[dc], stat_r.at[dc], along(dc))
        copy.start()
        stat_copies.append(copy)

    def pair_step(i, carry):
        at = pl.ds(pl.multiple_of(i * SLOT, SLOT), SLOT)
        s_ref[at, :] = dot(take_rows(sc_ref, at).astype(BF16), xt[i], NT)
        return carry

    lax.fori_loop(0, half, pair_step, 0)

    width = CH + 4 * PV + channels
    wnorm[...] = jnp.zeros(wnorm.shape, F32)
    for h in range(heads):
        hs, k = divmod(h, heads_local)
        wsmall[h * SMALL : (h + 1) * SMALL] = wo2[hs, k * width : k * width + SMALL]
        tail = wo2[hs, k * width + SMALL - 16 : k * width + SMALL].astype(F32)
        wnorm[h * PV : (h + 1) * PV] = tail[16 - PV :]
    nq = nq_ref[...].astype(F32)
    for k in range(S * C):
        nq3[k] = nq[k * share : (k + 1) * share]

    own_top, own_total = stat_send[0:SLOT, :], stat_send[SLOT:, :]
    for copy in stat_copies:
        copy.wait()
    all_top = own_top
    for dc in range(1, C):
        all_top = jnp.maximum(all_top, stat_recv[dc, 0:SLOT])
    all_total = own_total * jnp.exp(own_top - all_top)
    for dc in range(1, C):
        all_total = all_total + stat_recv[dc, SLOT:] * jnp.exp(stat_recv[dc, 0:SLOT] - all_top)
    live = lax.broadcasted_iota(jnp.int32, all_total.shape, 0) < heads
    factor = jnp.where(live, jnp.exp(own_top - all_top) / jnp.where(live, all_total, 1.0), 0.0)
    padb[...] = jnp.zeros(padb.shape, F32)
    padb[0:SLOT] = factor
    factor_columns = padb[...].T[0:half]

    fmat[...] = jnp.zeros(fmat.shape, F32)
    lpmat[...] = jnp.zeros(lpmat.shape, F32)
    for h in range(heads):
        f = factor[h : h + 1, 0:half]
        ft = f * own_total[h : h + 1, 0:half]
        at = h * SMALL
        fmat[at : at + CH, 0:half] = pv_ref[h, 0:CH] * f
        moved = []
        for a in range(3):
            p = pv_ref[h, CH + a * PV : CH + (a + 1) * PV]
            moved.append(p * f - qt[a : a + 1] * ft)
        for b in range(3):
            local = qr[0][b] * moved[0] + qr[1][b] * moved[1] + qr[2][b] * moved[2]
            fmat[at + CH + b * PV : at + CH + (b + 1) * PV, 0:half] = local
            lpmat[b * 128 + h * PV : b * 128 + (h + 1) * PV, 0:half] = local
    small = fmat[...].T[0:half, 0 : heads * SMALL].astype(BF16)
    projected = dot(small, wsmall[...])
    for h in range(heads):
        hs, k = divmod(h, heads_local)
        part = s_ref[pl.ds(h, half, stride=SLOT), :] * factor_columns[:, h : h + 1]
        projected = projected + dot(
            part.astype(BF16), wo2[hs, k * width + SMALL : (k + 1) * width]
        )
    points = lpmat[...].T[0:half]
    feat = projected.shape[1]
    for c in range(C):
        psend[c, :, 0:feat] = projected[c * share : (c + 1) * share].astype(BF16)
        psend[c, :, feat:] = points[c * share : (c + 1) * share].astype(BF16)
    red_copies = []
    for dc in range(1, C):
        copy = remote(
            psend.at[lax.rem(col + dc, C)], precv.at[dc], red_s.at[dc], red_r.at[dc], along(dc)
        )
        copy.start()
        red_copies.append(copy)
    for copy in ffn_copies:
        copy.wait()
    total = psend[col].astype(F32)
    for dc in range(1, C):
        red_copies[dc - 1].wait()
        total = total + precv[dc].astype(F32)
    x0, x1, x2 = total[:, feat : feat + 128], total[:, feat + 128 : feat + 256], total[:, feat + 256 :]
    norms = jnp.sqrt(1.0 + x0 * x0 + x1 * x1 + x2 * x2).astype(BF16)
    projected = total[:, 0:feat] + dot(norms, wnorm[...].astype(BF16))
    first = layer_norm(nq3[s * C + col] + projected, g1_ref[...])
    rounded = first.astype(BF16)
    gated = dot(rounded, gate[...])
    hidden = (gated / (1.0 + jnp.exp(-gated)) * dot(rounded, up[...])).astype(BF16)
    fresh = layer_norm(first + dot(hidden, down[...]), g2_ref[...]).astype(BF16)
    nsend[...] = fresh
    nodes_ref[s * C + col] = fresh
    ag_copies = []
    for dc in range(1, C):
        copy = remote(nsend, nodes_ref.at[s * C + col], ag_s.at[dc], ag_r.at[dc], along(dc))
        copy.start()
        ag_copies.append(copy)
    for copy in ag_copies:
        copy.wait()
    node_copy = remote(
        nodes_ref.at[pl.ds(s * C, C)], nodes_ref.at[pl.ds(s * C, C)],
        node_s.at[0], node_r.at[0], {"sub": other},
    )
    node_copy.start()
    eqf[...] = jnp.zeros(eqf.shape, F32)
    for c in range(C):
        eqf[c * share : (c + 1) * share] = dot(nodes_ref[s * C + c], weq_ref[...])
    eqt = eqf[...].T[:, 0:half]
    hi = eqt.astype(BF16)
    lo = (eqt - hi.astype(F32)).astype(BF16)
    lhs_in[:, channels : channels + 2 * half] = jnp.concatenate([hi, lo], axis=1)

    index = lax.broadcasted_iota(jnp.int32, (2 * half, kcount), 0)
    out_copies = []
    for b in range(blocks):
        for i in range(ROWS):
            block = xt[b * ROWS + i]
            at = b * ROWS + i
            mark = ((index == at) | (index == at + half)).astype(F32).astype(BF16)
            edge = dot(lhs_in[...], jnp.concatenate([block, mark], axis=0)) + ekt[...]
            edge = jnp.maximum(edge, 0.0).astype(BF16)
            put_rows(
                xf, pl.ds(i, channels, stride=ROWS), block.astype(F32) + dot(lhs_out[...], edge)
            )
        ostage[b] = take_rows(xf, own_rows).reshape(cs, ROWS, kcount).astype(BF16)
        rstage[b] = take_rows(xf, other_rows).reshape(cs, ROWS, kcount).astype(BF16)
        window = pairs_ref.at[:, pl.ds(s * half + b * ROWS, ROWS), :]
        copy = remote(rstage.at[b], window, o_s.at[b], o_r.at[b], {"sub": other})
        copy.start()
        out_copies.append(copy)
        copy = pltpu.make_async_copy(ostage.at[b], window, o_own.at[b])
        copy.start()
        out_copies.append(copy)
    for copy in out_copies:
        copy.wait()
    node_copy.wait()


def shards(
    node_query, query_angles, query_trans, query_chain, node_key, key_angles, key_trans,
    key_chain, pair_features, pair_mask, query_weight, key_weight, bias_weight, point_gain,
    chain_gain, out_weight, first_gain, second_gain, gate_weight, up_weight, down_weight,
    edge_query_weight, edge_key_weight, edge_in_weight, edge_out_weight,
):
    S, R, C = lax.axis_size("sub"), lax.axis_size("row"), lax.axis_size("col")
    qcount, features = node_query.shape
    kcount = key_angles.shape[1]
    half = qcount // S
    share = half // C
    cs = pair_features.shape[0]
    channels = cs * S
    heads_local = point_gain.shape[0]
    heads = heads_local * S
    blocks = half // ROWS
    hidden = edge_in_weight.shape[1]
    ffn = gate_weight.shape[1]
    kpad = -(-key_weight.shape[1] // 128) * 128
    qpad = -(-query_weight.shape[1] // 128) * 128
    small_rows = -(-heads * SMALL // 128) * 128
    group = R * S - 1
    dims = (S, R, C, heads_local, half, kcount, share, channels)
    vm = pl.BlockSpec(memory_space=pltpu.VMEM)
    anyspace = pl.BlockSpec(memory_space=pl.ANY)
    in_specs = [vm] * 8 + [anyspace] + [vm] * 9 + [anyspace] * 3 + [vm] * 4
    V = pltpu.VMEM
    DMA = pltpu.SemaphoreType.DMA
    scratch = [
        V((blocks, cs, ROWS, kcount), BF16),
        V((blocks, cs, ROWS, kcount), BF16),
        V((R * S, node_key.shape[0], features), BF16),
        V((S,) + query_weight.shape, BF16),
        V((S,) + key_weight.shape, BF16),
        V((S,) + bias_weight.shape, BF16),
        V((S, 1, heads_local), F32),
        V((S, 1, heads_local), F32),
        V((S,) + out_weight.shape, BF16),
        V(gate_weight.shape, BF16),
        V(up_weight.shape, BF16),
        V(down_weight.shape, BF16),
        V((kcount, kpad), F32),
        V((qcount, qpad), F32),
        V((128, 128), F32),
        V((heads, DEPTH, half), F32),
        V((heads, DEPTH, kcount), F32),
        V((heads, CH, kcount), BF16),
        V((heads, 3 * PV, kcount), F32),
        V((hidden, kcount), F32),
        V((hidden, channels + 2 * half), BF16),
        V((channels, hidden), BF16),
        V((kcount // 128, channels * ROWS, 128), F32),
        V((half, channels, kcount), BF16),
        V((kcount // 128, half * SLOT, 128), F32),
        V((heads, CH + 3 * PV, half), F32),
        V((half * SLOT, channels), F32),
        V((2 * SLOT, 128), F32),
        V((C, 2 * SLOT, 128), F32),
        V((small_rows, 128), F32),
        V((384, 128), F32),
        V((heads * SMALL, features), BF16),
        V((128, features), F32),
        V((S * C, share, features), F32),
        V((C, share, features + 384), BF16),
        V((C, share, features + 384), BF16),
        V((share, features), BF16),
        V((128, hidden), F32),
        V((blocks, cs, ROWS, kcount), BF16),
        V((blocks, cs, ROWS, kcount), BF16),
    ] + [
        DMA((n,))
        for n in (blocks, blocks, blocks, group, group, 6, 6, 3, C, C, C, C, C, C, 1, 1,
                  blocks, blocks, blocks)
    ]
    nodes, pairs = pl.pallas_call(
        functools.partial(kernel, dims),
        out_shape=(
            jax.ShapeDtypeStruct((S * C, share, features), BF16),
            jax.ShapeDtypeStruct(pair_features.shape, BF16),
        ),
        in_specs=in_specs,
        out_specs=(vm, anyspace),
        scratch_shapes=scratch,
        compiler_params=pltpu.CompilerParams(
            collective_id=0, has_side_effects=True, vmem_limit_bytes=60 * 1024 * 1024
        ),
    )(
        node_query, query_angles, query_trans, query_chain.reshape(1, qcount), node_key,
        key_angles, key_trans, key_chain.reshape(1, kcount), pair_features, pair_mask,
        query_weight, key_weight, bias_weight, point_gain.reshape(1, heads_local),
        chain_gain.reshape(1, heads_local), out_weight, first_gain.reshape(1, features),
        second_gain.reshape(1, features), gate_weight, up_weight, down_weight,
        edge_query_weight, edge_key_weight, edge_in_weight, edge_out_weight,
    )
    return nodes.reshape(qcount, features), pairs


def solution(mesh):
    return jax.shard_map(
        shards,
        mesh=mesh,
        in_specs=(
            P(("rep", "row"), None),
            P(None, ("rep", "row")),
            P(None, ("rep", "row")),
            P(("rep", "row")),
            P(("rep", "col", "row", "sub"), None),
            P(None, ("rep", "col")),
            P(None, ("rep", "col")),
            P(("rep", "col")),
            P("sub", ("rep", "row"), "col"),
            P(("rep", "row"), "col"),
            P(None, "sub"),
            P(None, "sub"),
            P(None, "sub"),
            P("sub"),
            P("sub"),
            P("sub", None),
            P(),
            P(),
            P(),
            P(),
            P(),
            P(),
            P(),
            P(),
            P(),
        ),
        out_specs=(P(("rep", "row"), None), P("sub", ("rep", "row"), "col")),
        check_vma=False,
    )
```

time: 187 us -> 69.6 us (0.37)
  matrix products: 59.1 us -> 0 us
  Pallas kernels: 0 us -> 57.7 us
  waiting for transfers between devices: 36.7 us -> 0 us
  blocking collectives: 35.5 us -> 0 us
  local copies, waits for them, and re-layouts: 35.9 us -> 11 us
  between operations: 14.5 us -> 0.64 us
  other arithmetic: 4.1 us -> 0 us
    dot_general x21 -> x0, matrix products: 59.1 us -> none  [the longest x5 26.7 us: leading_product(): lax.dot_general(left, right, (((0,), (0,)), ((), ())), preferred_element_...]
    pallas_call x0 -> x1, Pallas kernels: none -> 57.7 us  [shards(): pl.pallas_call(functools.partial(kernel, dims), out_shape=(jax.ShapeDtype...]
    reduce_scatter x1 -> x0, waiting for transfers between devices: 27.6 us -> none  [node_section(): lax.psum_scatter(sums, 'col', scatter_dimension=0, tiled=True)]
    all_gather x2 -> x0, blocking collectives: 19.7 us -> none  [the longest x1 13.2 us: node_section(): return lax.all_gather(node_share, 'col', axis=0, tiled=True)]
    pmax x1 -> x0, blocking collectives: 12.4 us -> none  [attend(): row_max = lax.pmax(jnp.max(scores, axis=2), 'col')]
    unnamed x4 -> x0, waiting for transfers between devices: 9.05 us -> none
    reshape x10 -> x0, local copies, waits for them, and re-layouts: 6.82 us -> none  [the longest x2 3.6 us: attend(): key_proj[:, :, 2 * CH + 3 * PQ:].reshape(key_count, heads, 3, PV)]
    dynamic_update_slice x4 -> x0, local copies, waits for them, and re-layouts: 6.24 us -> none  [edge_step(): return lax.dynamic_update_slice_in_dim(result, fresh, begin, 1)]
  transfers between devices with their start and end apart: 3 -> 0, of which waited for: 2 -> 0; matrix products, arithmetic and copies ran while one was open for 25% -> 0% of each run, Pallas kernels for 0% -> 0%
where the time goes in v1:
time: 69.6 us; the launch traced here: 69.3 us
  Pallas kernels  57.7 us (83%)
  local copies, waits for them, and re-layouts  11 us (16%)
    pallas_call x1, Pallas kernels, shards(): pl.pallas_call(functools.partial(kernel, dims), out_shape=(jax.ShapeDtype...  57.7 us
    unnamed x5, local copies, waits for them, and re-layouts  11 us

profile of v1, /device:TPU:0, one launch (start us, length us, event | category | flops | bytes accessed | tf_op | source)
XLA Modules:
  0.0 69.3 jit_solution(15469280834685153658)
XLA Ops:
  0.6 1.4 %copy.29.wb_ref = bf16[128,6]{1,0:T(8,128)(2,1)} copy(bf16[128,6]{0,1:T(8,128)(2,1)} %param.37) | data formatting | bytes 3072 | tf_op args[12]
  2.0 1.6 %copy.27.wq_ref = bf16[256,168]{1,0:T(8,128)(2,1)} copy(bf16[256,168]{0,1:T(8,128)(2,1)} %param.35) | data formatting | bytes 172032 | tf_op args[10]
  3.7 1.8 %copy.28.wk_ref = bf16[256,408]{1,0:T(8,128)(2,1)} copy(bf16[256,408]{0,1:T(8,128)(2,1)} %param.36) | data formatting | bytes 417792 | tf_op args[11]
  5.5 57.7 %shard_map.248 = (bf16[8,16,256]{2,1,0:T(8,128)(2,1)}, bf16[64,128,256]{2,1,0:T(8,128)(2,1)}) custom-call(bf16[128,256]{1,0:T(8,128)(2,1)} %nq_ref.1, f32[3,128]{1,0:T(4,128)} %qa_ref.1, f32[3,128]{1,0:T(4,128)} %qt_ref.1, s32[1,128]{1,0:T(1,128)} %bitcast.11, bf16[64,256]{1,0:T(8,128)(2,1)} %nk_ref.1, f32[3,256]{1,0:T(4,128)} %ka_ref.1, f32[3,256]{1,0:T(4,128)} %kt_ref.1, ...), custom_call_target="tpu_custom_call" | custom-call | tf_op jit(solution)/shard_map/pallas_call | solution.py:465
  63.1 1.5 %copy.32 = bf16[128,256]{1,0:T(8,128)(2,1)} copy(bf16[128,256]{1,0:T(8,128)(2,1)} %bitcast.7) | data formatting | bytes 131072
  64.6 4.7 %copy.33 = bf16[64,128,256]{2,1,0:T(8,128)(2,1)} copy(bf16[64,128,256]{2,1,0:T(8,128)(2,1)} %get-tuple-element.9) | data formatting | bytes 8388608
